TPU v7x, 32 devices: a whole 2x2x4 slice. The times are simulated.
32 devices in a mesh: grp: 2 (over y), smp: 4 (over x, core), row: 4 (over z).
Axes of the slice: x: 2, y: 2, z: 4, core: 2. Of those that a mesh axis runs over, the one named last changes fastest.
Arguments:
- positions: float32 [8, 3, 4096], P(('grp', 'smp'), None, 'row'), parts along dimension 0, may hold values from -60 to 60
- noise_draw: float32 [8, 3, 4096], P(('grp', 'smp'), None, 'row'), parts along dimension 0, may hold values from -6 to 6
- noise_level: float32 [8], P(('grp', 'smp')), parts along dimension 0, may hold values from 0.5 to 80
- atom_single: bfloat16 [8192, 128], P(('grp', 'row')), parts along dimension 0, may hold values from -6 to 6
- token_single: bfloat16 [1024, 768], P(('grp', 'row')), parts along dimension 0, may hold values from -6 to 6
- pair_cond: bfloat16 [1024, 512, 128], P(('grp', 'row'), 'smp'), parts along dimension 0, may hold values from -6 to 6
- atom_to_token: int32 [8192], P(('grp', 'row')), parts along dimension 0, may hold values from 0 to 511, as said below
- window_offsets: int32 [256], P(('grp', 'row')), parts along dimension 0, may hold values from -96 to 0
- atom_mask: int32 [8192], P('grp'), parts along dimension 0, may hold values 0 or 1
- token_mask: int32 [1024], P('grp'), parts along dimension 0, may hold values 0 or 1
- coord_in: float32 [3, 128], replicated, may hold values from -3.5 to 3.5
- atom_gain: float32 [2, 128], replicated, may hold values from 0.1 to 1.9
- atom_qkv: bfloat16 [2, 128, 384], replicated, may hold values from -1 to 1
- atom_proj: bfloat16 [2, 128, 128], replicated, may hold values from -0.5 to 0.5
- gather_in: bfloat16 [128, 768], replicated, may hold values from -0.5 to 0.5
- noise_embed: float32 [768], replicated, may hold values from -6 to 6
- pair_gain: float32 [128], replicated, may hold values from 0.1 to 1.9
- pair_heads: bfloat16 [128, 16], replicated, may hold values from -0.5 to 0.5
- token_gain: float32 [2, 768], replicated, may hold values from 0.1 to 1.9
- token_qkv: bfloat16 [768, 2304], replicated, may hold values from -1 to 1
- token_proj: bfloat16 [768, 768], replicated, may hold values from -0.21875 to 0.21875
- ffn_in: bfloat16 [768, 3072], replicated, may hold values from -0.21875 to 0.21875
- ffn_out: bfloat16 [1536, 768], replicated, may hold values from -0.15625 to 0.15625
- scatter_out: bfloat16 [768, 128], replicated, may hold values from -0.21875 to 0.21875
- out_gain: float32 [128], replicated, may hold values from 0.1 to 1.9
- coord_out: bfloat16 [3, 128], replicated, may hold values from -0.5 to 0.5
Outputs:
- token_out: bfloat16 [8, 512, 768], P(('grp', 'smp'), 'row'), parts along dimension 0
- direction: float32 [8, 3, 4096], P(('grp', 'smp'), None, 'row'), parts along dimension 0
There are 2 independent parts, one for each index of `grp`. A program takes and returns all parts, laid end to end along the dimension named above; an argument that names none is the same for every part. Nothing has to cross between parts.
Inputs may be any that keep to these rules, and one draw needn't show every extreme that they name: `atom_to_token`: never falls along the atoms; atoms k * 1024 to (k + 1) * 1024 - 1 belong to tokens k * 128 to (k + 1) * 128 - 1; some tokens have no atom.
All inputs are finite; a program needn't handle non-finite values.
Results may differ from a plain program's by a relative error of at most 0.013.
Values may be sent and summed in bfloat16 or wider, within the bound.
A program may use at most 128 MiB of HBM per device.

v0:
```python
import jax
import jax.numpy as jnp
from jax import lax
from jax.sharding import PartitionSpec as P

D = 768
HEADS = 16
FF = 1536
CA = 128
AHEADS = 4
WQ = 32
WK = 128
HALO = 96
sigma_data = 16.0
gamma_boost = 0.8
norm_eps = 1e-05
masked_score = -1e30
outside_score = -2e30


def with_halo(block, sides, width):
    for axis, dim in sides:
        count = lax.axis_size(axis)
        forward = [(i, i + 1) for i in range(count - 1)]
        backward = [(target, source) for source, target in forward]
        low = lax.ppermute(
            lax.slice_in_dim(block, block.shape[dim] - width, None, axis=dim), axis, forward
        )
        high = lax.ppermute(lax.slice_in_dim(block, 0, width, axis=dim), axis, backward)
        block = jnp.concatenate([low, block, high], axis=dim)
    return block


def layer_norm(values, norm_gain):
    average = jnp.mean(values, axis=-1, keepdims=True)
    centred = values - average
    variance = jnp.mean(centred * centred, axis=-1, keepdims=True)
    return centred * lax.rsqrt(variance + norm_eps) * norm_gain


def softmax_rows(scores):
    largest = jnp.max(scores, axis=-1, keepdims=True)
    exponent = jnp.exp(scores - largest)
    return exponent / jnp.sum(exponent, axis=-1, keepdims=True)


def pair_bias_of(pair_tile, pair_gain, pair_heads):
    normed = layer_norm(pair_tile.astype(jnp.float32), pair_gain).astype(jnp.bfloat16)
    return jnp.einsum("ijc,ch->hij", normed, pair_heads, preferred_element_type=jnp.float32).astype(
        jnp.bfloat16
    )


def block_spans(extended, block_count, span_blocks):
    tail_shape = extended.shape[1:]
    grouped = extended.reshape((block_count + span_blocks - 1, WQ) + tail_shape)
    pieces = [grouped[shift : shift + block_count] for shift in range(span_blocks)]
    return jnp.stack(pieces, axis=1).reshape((block_count, span_blocks * WQ) + tail_shape)


def window_attend(queries, windows, live, inside, w_out):
    block_count = queries.shape[0] // WQ
    head_size = CA // AHEADS
    span_rows = windows.shape[1]
    query_heads = queries.reshape(block_count, WQ, AHEADS, head_size)
    key_heads = windows[:, :, :CA].reshape(block_count, span_rows, AHEADS, head_size)
    value_heads = windows[:, :, CA:].reshape(block_count, span_rows, AHEADS, head_size)
    scores = jnp.einsum(
        "bqhd,bkhd->bhqk", query_heads, key_heads, preferred_element_type=jnp.float32
    ) / jnp.sqrt(jnp.float32(head_size))
    scores = jnp.where(live[:, None, None, :], scores, masked_score)
    scores = jnp.where(inside[:, None, None, :], scores, outside_score)
    weights = softmax_rows(scores).astype(jnp.bfloat16)
    mixed_heads = jnp.einsum(
        "bhqk,bkhd->bqhd", weights, value_heads, preferred_element_type=jnp.float32
    ).astype(jnp.bfloat16)
    return jnp.dot(
        mixed_heads.reshape(block_count * WQ, CA), w_out, preferred_element_type=jnp.float32
    )


def atom_block(atom_state, norm_gain, w_qkv, w_out, offsets, live_ext):
    row_count = atom_state.shape[0]
    normed = layer_norm(atom_state, norm_gain).astype(jnp.bfloat16)
    widened = with_halo(normed, (("row", 0),), HALO)
    projected = jnp.dot(widened, w_qkv, preferred_element_type=jnp.float32).astype(jnp.bfloat16)
    queries = projected[HALO : HALO + row_count, :CA]
    extended = projected[:, CA:]
    block_count = row_count // WQ
    span_blocks = (2 * HALO + WQ) // WQ
    windows = block_spans(extended, block_count, span_blocks)
    live = block_spans(live_ext, block_count, span_blocks) > 0
    relative = jnp.arange(span_blocks * WQ, dtype=jnp.int32)[None, :]
    first_key = offsets[:, None] + HALO
    inside = (relative >= first_key) & (relative < first_key + WK)
    return atom_state + window_attend(queries, windows, live, inside, w_out)


def per_device(
    positions,
    noise_draw,
    noise_level,
    atom_single,
    token_single,
    pair_cond,
    atom_to_token,
    window_offsets,
    atom_mask,
    token_mask,
    coord_in,
    atom_gain,
    atom_qkv,
    atom_proj,
    gather_in,
    noise_embed,
    pair_gain,
    pair_heads,
    token_gain,
    token_qkv,
    token_proj,
    ffn_in,
    ffn_out,
    scatter_out,
    out_gain,
    coord_out,
):
    row_index = lax.axis_index("row")
    tok_rows = token_single.shape[0]
    atom_rows = atom_single.shape[0]
    head_size = D // HEADS
    biases = lax.all_gather(
        pair_bias_of(pair_cond, pair_gain, pair_heads), "smp", axis=2, tiled=True
    )
    local_token = atom_to_token - row_index * tok_rows
    valid_local = lax.dynamic_slice_in_dim(atom_mask, row_index * atom_rows, atom_rows)
    member = (local_token[None, :] == jnp.arange(tok_rows, dtype=jnp.int32)[:, None]) & (
        valid_local[None, :] > 0
    )
    onehot = member.astype(jnp.bfloat16)
    counts = jnp.maximum(jnp.sum(member.astype(jnp.float32), axis=1), 1.0)
    live_padded = jnp.pad(atom_mask, (HALO, HALO))
    live_ext = lax.dynamic_slice_in_dim(live_padded, row_index * atom_rows, atom_rows + 2 * HALO)
    key_live = token_mask > 0
    coords = positions[0]
    kicks = noise_draw[0]
    level_now = noise_level[0]
    level_hat = (1.0 + gamma_boost) * level_now
    noisy = coords + jnp.sqrt(level_hat * level_hat - level_now * level_now) * kicks
    scaled = noisy / jnp.sqrt(level_hat * level_hat + sigma_data * sigma_data)
    atom_state = atom_single.astype(jnp.float32) + jnp.einsum(
        "ka,kc->ac", scaled, coord_in, precision=lax.Precision.HIGHEST
    )
    atom_state = atom_block(
        atom_state, atom_gain[0], atom_qkv[0], atom_proj[0], window_offsets, live_ext
    )
    lifted = jax.nn.relu(
        jnp.dot(atom_state.astype(jnp.bfloat16), gather_in, preferred_element_type=jnp.float32)
    ).astype(jnp.bfloat16)
    pooled = jnp.dot(onehot, lifted, preferred_element_type=jnp.float32) / counts[:, None]
    token_state = (
        pooled
        + token_single.astype(jnp.float32)
        + jnp.log(level_hat / sigma_data) / 4.0 * noise_embed
    )
    normed = layer_norm(token_state, token_gain[0]).astype(jnp.bfloat16)
    projected = jnp.dot(normed, token_qkv, preferred_element_type=jnp.float32).astype(jnp.bfloat16)
    gathered = lax.all_gather(projected[:, D:], "row", axis=0, tiled=True)
    key_count = gathered.shape[0]
    query_heads = projected[:, :D].reshape(tok_rows, HEADS, head_size)
    key_heads = gathered[:, :D].reshape(key_count, HEADS, head_size)
    value_heads = gathered[:, D:].reshape(key_count, HEADS, head_size)
    scores = jnp.einsum(
        "ihd,jhd->hij", query_heads, key_heads, preferred_element_type=jnp.float32
    ) / jnp.sqrt(jnp.float32(head_size))
    scores = scores + biases.astype(jnp.float32)
    scores = jnp.where(key_live[None, None, :], scores, masked_score)
    weights = softmax_rows(scores).astype(jnp.bfloat16)
    mixed_heads = (
        jnp.einsum("hij,jhd->ihd", weights, value_heads, preferred_element_type=jnp.float32)
        .astype(jnp.bfloat16)
        .reshape(tok_rows, D)
    )
    token_state = token_state + jnp.dot(mixed_heads, token_proj, preferred_element_type=jnp.float32)
    normed = layer_norm(token_state, token_gain[1]).astype(jnp.bfloat16)
    hidden = jnp.dot(normed, ffn_in, preferred_element_type=jnp.float32)
    active = (jax.nn.silu(hidden[:, :FF]) * hidden[:, FF:]).astype(jnp.bfloat16)
    token_state = token_state + jnp.dot(active, ffn_out, preferred_element_type=jnp.float32)
    token_result = token_state.astype(jnp.bfloat16)
    spread_back = jnp.dot(token_result, scatter_out, preferred_element_type=jnp.float32).astype(
        jnp.bfloat16
    )
    atom_state = atom_state + lax.dot_general(
        onehot, spread_back, (((0,), (0,)), ((), ())), preferred_element_type=jnp.float32
    )
    atom_state = atom_block(
        atom_state, atom_gain[1], atom_qkv[1], atom_proj[1], window_offsets, live_ext
    )
    normed_out = layer_norm(atom_state, out_gain).astype(jnp.bfloat16)
    update = lax.dot_general(
        coord_out, normed_out, (((1,), (1,)), ((), ())), preferred_element_type=jnp.float32
    )
    base_square = sigma_data * sigma_data + level_hat * level_hat
    skip_scale = sigma_data * sigma_data / base_square
    out_scale = level_hat * sigma_data / jnp.sqrt(base_square)
    denoised = skip_scale * noisy + out_scale * update
    direction = (noisy - denoised) / level_hat
    return (token_result[None], direction[None])


def solution(mesh):
    in_specs = (
        P(("grp", "smp"), None, "row"),
        P(("grp", "smp"), None, "row"),
        P(("grp", "smp")),
        P(("grp", "row"), None),
        P(("grp", "row"), None),
        P(("grp", "row"), "smp", None),
        P(("grp", "row")),
        P(("grp", "row")),
        P("grp"),
        P("grp"),
        P(),
        P(),
        P(),
        P(),
        P(),
        P(),
        P(),
        P(),
        P(),
        P(),
        P(),
        P(),
        P(),
        P(),
        P(),
        P(),
    )
    out_specs = (P(("grp", "smp"), "row", None), P(("grp", "smp"), None, "row"))
    return jax.shard_map(
        per_device, mesh=mesh, in_specs=in_specs, out_specs=out_specs, check_vma=False
    )
```

profile of v0, /device:TPU:0, one launch (start us, length us, event | category | flops | bytes accessed | tf_op | source)
XLA Modules:
  0.0 203.9 jit_solution(14690072002025671553)
XLA Ops:
  8.1 2.2 %fusion.123 = (f32[1024]{0:T(1024)S(1)}, f32[1024,128]{1,0:T(8,128)S(1)}) fusion(f32[3,128]{1,0:T(4,128)} %param.36, f32[]{:T(128)S(6)} %sqrt.8, f32[1,3,1024]{2,0,1:T(1,128)} %param.27, f32[]{:T(128)S(6)} %sqrt.7, f32[1,3,1024]{2,0,1:T(1,128)} %param.26, bf16[1024,128]{1,0:T(8,128)(2,1)} %param.29), kind=kOutput, calls=%fused_computation.202 | convolution fusion | flops 5120000 | bytes 816648 | tf_op jit(solution)/shard_map/ka,kc->ac/dot_general | solution.py:150
  10.7 1.3 slice_bitcast_fusion
  12.4 0.7 copy-done.10
  13.7 5.6 %collective-permute-start = (bf16[96,128]{1,0:T(8,128)(2,1)}, bf16[96,128]{1,0:T(8,128)(2,1)}, u32[]{:S(2)}, u32[]{:S(2)}) collective-permute-start(bf16[96,128]{1,0:T(8,128)(2,1)} %get-tuple-element.32), channel_id=1, source_target_pairs={{0,1},{1,2},{2,3},{4,5},{5,6},{6,7},{8,9},{9,10},{10,11},{12,13},{... | collective-permute-start | bytes 73736 | tf_op jit(solution)/shard_map/ppermute | solution.py:26
  19.3 1.3 collective-permute-start.1
  20.6 1.7 pad_dynamic-slice_fusion.6
  22.2 0.8 stack.88
  23.0 1.4 stack.89
  24.4 1.4 stack.90
  25.7 1.4 stack.91
  27.1 1.4 stack.92
  28.5 1.4 stack.93
  29.8 1.4 stack.94
  31.2 1.6 stack.95
  32.8 1.5 broadcast_compare_fusion
  34.3 0.7 broadcast_add_fusion.1
  35.0 0.7 dynamic-slice_compare_fusion
  35.7 0.7 broadcast_subtract_fusion
  37.1 0.7 fusion.94
  37.8 1.3 broadcast_multiply_fusion.1
  39.1 0.8 slice_reduce_fusion
  39.9 1.5 gt.27
  41.4 1.4 convolution_convert_fusion.2
  43.0 0.7 slice.290
  44.1 2.5 %fusion.117 = (bf16[32,224,128]{2,1,0:T(8,128)(2,1)}, bf16[32,224,128]{2,1,0:T(8,128)(2,1)}) fusion(bf16[32,224,256]{2,1,0:T(8,128)(2,1)S(1)} %bitcast.141), kind=kLoop, calls=%fused_computation.196 | loop fusion | bytes 7340032 | tf_op jit(solution)/shard_map/slice | solution.py:66
  46.5 4.0 %copy.78 = bf16[32,224,128]{1,2,0:T(8,128)(2,1)} copy(bf16[32,224,128]{2,1,0:T(8,128)(2,1)} %get-tuple-element.12) | data formatting | bytes 3670016 | tf_op jit(solution)/shard_map/slice | solution.py:66
  50.5 2.7 %reshape.297 = bf16[32,32,4,32]{3,2,1,0:T(4,128)(2,1)} reshape(bf16[1024,128]{1,0:T(8,128)(2,1)} %slice.290) | data formatting | bytes 524288 | tf_op jit(solution)/shard_map/reshape | solution.py:65
  53.3 3.9 %copy.77 = bf16[32,224,128]{1,2,0:T(8,128)(2,1)} copy(bf16[32,224,128]{2,1,0:T(8,128)(2,1)} %get-tuple-element.13) | data formatting | bytes 3670016 | tf_op jit(solution)/shard_map/slice | solution.py:67
  57.2 2.6 %fusion.49 = f32[32,4,32,224]{3,2,1,0:T(8,128)S(1)} fusion(bf16[32,224,4,32]{1,3,2,0:T(8,128)(2,1)} %bitcast.139, bf16[32,32,4,32]{3,2,1,0:T(4,128)(2,1)} %reshape.297), kind=kOutput, calls=%fused_computation.72 | convolution fusion | flops 58720256 | bytes 5767168 | tf_op jit(solution)/shard_map/bqhd,bkhd->bhqk/dot_general | solution.py:68
  59.9 6.4 %fusion.124 = (f32[32,4,32]{2,1,0:T(4,128)S(1)}, f32[32,4,32,224]{3,2,1,0:T(8,128)S(1)}) fusion(f32[32,4,32,224]{3,2,1,0:T(8,128)S(1)} %fusion.49, pred[32,224]{1,0:T(8,128)(4,1)S(1)} %copy-done.17, pred[32,224]{1,0:T(8,128)(4,1)S(1)} %copy-done.19), kind=kOutput, calls=%fused_computation.203 | output fusion | flops 7340255 | bytes 7370752 | tf_op jit(solution)/shard_map/sub | solution.py:43
  66.3 1.0 fusion.35
  67.3 1.7 copy.80
  69.0 2.9 %reshape.299 = bf16[1024,128]{0,1:T(8,128)(2,1)} reshape(bf16[32,32,4,32]{1,0,3,2:T(8,128)(2,1)} %copy.80) | data formatting | bytes 524288 | tf_op jit(solution)/shard_map/reshape | solution.py:78
  71.9 2.2 %convolution_add_fusion.2 = f32[1024,128]{1,0:T(8,128)} fusion(f32[1024,128]{1,0:T(8,128)} %copy-done.3, bf16[1024,128]{0,1:T(8,128)(2,1)} %reshape.299, bf16[2,128,128]{2,1,0:T(8,128)(2,1)} %param.39), kind=kOutput, calls=%fused_computation.53 | convolution fusion | flops 33685504 | bytes 1343488 | tf_op jit(solution)/shard_map/dot_general | solution.py:77
  74.1 3.3 %fusion.125 = (f32[128]{0:T(128)}, f32[128,768]{1,0:T(8,128)}) fusion(f32[768]{0:T(1024)} %broadcast_multiply_fusion.1, bf16[128,768]{1,0:T(8,128)(2,1)} %param.30, f32[128]{0:T(128)} %broadcast_maximum_fusion, bf16[128,768]{1,0:T(8,128)(2,1)} %param.40, f32[1024,128]{1,0:T(8,128)} %convolution_add_fusion.2, s32[1024]{0:T(1024)S(1)} %broadcast_subtract_fusion, ...), kind=kOutput, calls=%fused_computation.204 | convolution fusion | flops 405110656 | bytes 1319936 | tf_op jit(solution)/shard_map/dot_general | solution.py:159
  77.5 0.7 broadcast_multiply_fusion.6
  78.1 1.2 multiply_reduce_fusion.4
  79.3 1.7 convolution_convert_fusion
  81.0 0.8 copy-done.7
  81.8 0.8 slice.292
  82.9 3.5 %convert_reduce_fusion = f32[128,128]{1,0:T(8,128)S(1)} fusion(bf16[128,128,128]{2,1,0:T(8,128)(2,1)} %param.31), kind=kLoop, calls=%fused_computation.4 | loop fusion | flops 4177920 | bytes 4259840 | tf_op jit(solution)/shard_map/reduce_sum | solution.py:35
  86.5 4.8 %fusion.5 = f32[128,128]{1,0:T(8,128)S(1)} fusion(bf16[128,128,128]{2,1,0:T(8,128)(2,1)S(1)} %copy-done.2, f32[128,128]{1,0:T(8,128)S(1)} %broadcast_multiply_fusion), kind=kLoop, calls=%fused_computation.7 | loop fusion | flops 8372224 | bytes 4325376 | tf_op jit(solution)/shard_map/reduce_sum | solution.py:37
  91.3 5.8 %fusion.8 = bf16[128,128,16]{1,2,0:T(8,128)(2,1)S(1)} fusion(bf16[128,128,128]{2,1,0:T(8,128)(2,1)S(1)} %copy-done.2, f32[128]{0:T(128)S(1)} %copy-done.27, f32[128,128]{1,0:T(8,128)S(1)} %add_rsqrt_fusion, f32[128,128]{1,0:T(8,128)S(1)} %broadcast_multiply_fusion, bf16[128,16]{0,1:T(8,128)(2,1)S(1)} %copy-done.25), kind=kOutput, calls=%fused_computation.10 | convolution fusion | flops 77594624 | bytes 4854272 | tf_op jit(solution)/shard_map/ijc,ch->hij/dot_general | solution.py:49
  97.2 1.0 copy.124
  98.4 23.7 %all-gather.3.cloned.1.call-done = bf16[512,1536]{1,0:T(8,128)(2,1)} async-done(((bf16[128,1536]{1,0:T(8,128)(2,1)}), bf16[512,1536]{1,0:T(8,128)(2,1)}) %all-gather.3.cloned.1.call-update) | async-done | bytes 1572880 | tf_op jit(solution)/shard_map/all_gather | solution.py:167
  122.1 1.5 fusion.118
  124.1 21.2 %all-gather.5.cloned.1.call-done = bf16[16,128,512]{2,1,0:T(8,128)(2,1)} async-done(((bf16[16,128,128]{2,1,0:T(8,128)(2,1)}), bf16[16,128,512]{2,1,0:T(8,128)(2,1)}) %all-gather.5.cloned.1.call-update) | async-done | bytes 2097168 | tf_op jit(solution)/shard_map/all_gather | solution.py:131
  145.4 3.3 %fusion.128 = f32[16,128]{1,0:T(8,128)S(1)} fusion(bf16[16,128,512]{2,1,0:T(8,128)(2,1)} %all-gather.5.cloned.1.call-done, pred[512]{0:T(512)(128)(4,1)S(1)} %broadcast_compare_fusion.1, bf16[128,16,48]{0,2,1:T(8,128)(2,1)S(1)} %bitcast.165, bf16[512,16,48]{0,2,1:T(8,128)(2,1)S(1)} %bitcast.160), kind=kOutput, calls=%fused_computation.205 | convolution fusion | flops 106955264 | bytes 3088896 | tf_op jit(solution)/shard_map/sub | solution.py:43
  148.8 4.5 %fusion.40 = bf16[16,48,128]{2,1,0:T(8,128)(2,1)} fusion(bf16[512,16,48]{0,2,1:T(8,128)(2,1)S(1)} %bitcast.162, f32[16,128]{1,0:T(8,128)S(1)} %fusion.128, bf16[16,128,512]{2,1,0:T(8,128)(2,1)} %all-gather.5.cloned.1.call-done, pred[512]{0:T(512)(128)(4,1)} %copy-done.23, bf16[128,16,48]{0,2,1:T(8,128)(2,1)} %bitcast.166, bf16[512,16,48]{0,2,1:T(8,128)(2,1)S(1)} %bitcast.161), kind=kOutput, calls=%fused_computation.60 | convolution fusion | flops 208767488 | bytes 4071936 | tf_op jit(solution)/shard_map/hij,jhd->ihd/dot_general | solution.py:179
  153.3 1.4 fusion.129
  154.9 3.3 %fusion.79 = f32[128,3072]{1,0:T(8,128)S(1)} fusion(bf16[768,3072]{1,0:T(8,128)(2,1)} %param.47, f32[128,768]{1,0:T(8,128)S(1)} %get-tuple-element.52, f32[768]{0:T(1024)S(1)} %get-tuple-element.8, f32[128]{0:T(128)S(1)} %add_rsqrt_fusion.4, f32[128]{0:T(128)S(1)} %broadcast_multiply_fusion.5), kind=kOutput, calls=%fused_computation.110 | convolution fusion | flops 604372992 | bytes 6688768 | tf_op jit(solution)/shard_map/dot_general | solution.py:185
  160.6 3.4 %collective-permute-start.2 = (bf16[96,128]{1,0:T(8,128)(2,1)S(1)}, bf16[96,128]{1,0:T(8,128)(2,1)S(1)}, u32[]{:S(2)}, u32[]{:S(2)}) collective-permute-start(bf16[96,128]{1,0:T(8,128)(2,1)S(1)} %get-tuple-element.30), channel_id=1, source_target_pairs={{0,1},{1,2},{2,3},{4,5},{5,6},{6,7},{8,9},{9,10},{10,11},{12,13},{... | collective-permute-start | bytes 73736 | tf_op jit(solution)/shard_map/ppermute | solution.py:26
  164.0 1.5 collective-permute-start.3
  165.6 4.1 %collective-permute-done.3 = bf16[96,128]{1,0:T(8,128)(2,1)S(1)} collective-permute-done((bf16[96,128]{1,0:T(8,128)(2,1)S(1)}, bf16[96,128]{1,0:T(8,128)(2,1)S(1)}, u32[]{:S(2)}, u32[]{:S(2)}) %collective-permute-start.3) | collective-permute-done | bytes 24608 | tf_op jit(solution)/shard_map/ppermute | solution.py:29
  170.7 2.5 %fusion.116 = (bf16[32,224,128]{2,1,0:T(8,128)(2,1)}, bf16[32,224,128]{2,1,0:T(8,128)(2,1)}) fusion(bf16[32,224,256]{2,1,0:T(8,128)(2,1)S(1)} %bitcast.142), kind=kLoop, calls=%fused_computation.195 | loop fusion | bytes 7340032 | tf_op jit(solution)/shard_map/slice | solution.py:66
  173.2 3.2 %copy.93 = bf16[32,224,128]{1,2,0:T(8,128)(2,1)S(1)} copy(bf16[32,224,128]{2,1,0:T(8,128)(2,1)} %get-tuple-element.10) | data formatting | bytes 3670016 | tf_op jit(solution)/shard_map/slice | solution.py:66
  176.8 0.7 fusion.47
  177.5 4.3 %fusion.131 = (f32[32,4,32]{2,1,0:T(4,128)}, f32[32,4,32,224]{3,2,1,0:T(8,128)}) fusion(f32[32,4,32,224]{3,2,1,0:T(8,128)S(1)} %fusion.47, pred[32,224]{1,0:T(8,128)(4,1)S(1)} %copy-done.18, pred[32,224]{1,0:T(8,128)(4,1)S(1)} %copy-done.20), kind=kOutput, calls=%fused_computation.208 | output fusion | flops 7340255 | bytes 7370752 | tf_op jit(solution)/shard_map/sub | solution.py:43
  181.8 3.1 %copy.92 = bf16[32,224,128]{1,2,0:T(8,128)(2,1)} copy(bf16[32,224,128]{2,1,0:T(8,128)(2,1)S(1)} %copy-done.5) | data formatting | bytes 3670016 | tf_op jit(solution)/shard_map/slice | solution.py:67
  184.9 3.8 %fusion.36 = bf16[32,32,4,32]{1,3,2,0:T(8,128)(2,1)S(1)} fusion(bf16[32,224,4,32]{1,3,2,0:T(8,128)(2,1)} %bitcast.159, f32[32,4,32,224]{3,2,1,0:T(8,128)} %get-tuple-element.56, f32[32,4,32]{2,1,0:T(4,128)} %get-tuple-element.55), kind=kOutput, calls=%fused_computation.50 | convolution fusion | flops 60686336 | bytes 5783552 | tf_op jit(solution)/shard_map/bhqk,bkhd->bqhd/dot_general | solution.py:74
  188.7 1.7 copy.95
  190.4 2.9 %reshape.308 = bf16[1024,128]{0,1:T(8,128)(2,1)} reshape(bf16[32,32,4,32]{1,0,3,2:T(8,128)(2,1)} %copy.95) | data formatting | bytes 524288 | tf_op jit(solution)/shard_map/reshape | solution.py:78
  193.3 1.6 fusion.132
  195.3 1.2 fusion.46
  (110 shorter events, 8.6 us)
Async XLA Ops:
  7.2 72.2 %copy-start = (bf16[768,2304]{1,0:T(8,128)(2,1)S(1)}, bf16[768,2304]{1,0:T(8,128)(2,1)}, u32[]{:S(2)}) copy-start(bf16[768,2304]{1,0:T(8,128)(2,1)} %param.45) | copy-start | bytes 10616836
  7.2 114.9 %all-gather.3.cloned.1.call-start = ((), (), s32[]{:S(2)}) async-start(), calls=%async_computation | async-start | bytes 1966080 | tf_op jit(solution)/shard_map/all_gather | solution.py:167
  10.3 1.7 copy-start.3
  12.4 0.7 copy-start.10
  13.7 27.7 %collective-permute-start = (bf16[96,128]{1,0:T(8,128)(2,1)}, bf16[96,128]{1,0:T(8,128)(2,1)}, u32[]{:S(2)}, u32[]{:S(2)}) collective-permute-start(bf16[96,128]{1,0:T(8,128)(2,1)} %get-tuple-element.32), channel_id=1, source_target_pairs={{0,1},{1,2},{2,3},{4,5},{5,6},{6,7},{8,9},{9,10},{10,11},{12,13},{... | collective-permute-start | bytes 73736 | tf_op jit(solution)/shard_map/ppermute | solution.py:26
  19.3 22.1 %collective-permute-start.1 = (bf16[96,128]{1,0:T(8,128)(2,1)}, bf16[96,128]{1,0:T(8,128)(2,1)}, u32[]{:S(2)}, u32[]{:S(2)}) collective-permute-start(bf16[96,128]{1,0:T(8,128)(2,1)} %get-tuple-element.33), channel_id=1, source_target_pairs={{1,0},{2,1},{3,2},{5,4},{6,5},{7,6},{9,8},{10,9},{11,10},{13,12},{... | collective-permute-start | bytes 73736 | tf_op jit(solution)/shard_map/ppermute | solution.py:29
  57.2 2.6 %copy-start.17 = (pred[32,224]{1,0:T(8,128)(4,1)S(1)}, pred[32,224]{1,0:T(8,128)(4,1)}, u32[]{:S(2)}) copy-start(pred[32,224]{1,0:T(8,128)(4,1)} %gt.27) | copy-start | bytes 21508
  57.2 2.6 %copy-start.19 = (pred[32,224]{1,0:T(8,128)(4,1)S(1)}, pred[32,224]{1,0:T(8,128)(4,1)}, u32[]{:S(2)}) copy-start(pred[32,224]{1,0:T(8,128)(4,1)} %fusion.94) | copy-start | bytes 21508
  59.9 6.4 %copy-start.8 = (bf16[32,224,128]{1,2,0:T(8,128)(2,1)S(1)}, bf16[32,224,128]{1,2,0:T(8,128)(2,1)}, u32[]{:S(2)}) copy-start(bf16[32,224,128]{1,2,0:T(8,128)(2,1)} %copy.77) | copy-start | bytes 5505028
  81.0 0.8 copy-start.7
  82.7 8.6 %copy-start.25 = (bf16[128,16]{0,1:T(8,128)(2,1)S(1)}, bf16[128,16]{0,1:T(8,128)(2,1)}, u32[]{:S(2)}) copy-start(bf16[128,16]{0,1:T(8,128)(2,1)} %param.43) | copy-start | bytes 12292
  82.7 8.6 %copy-start.27 = (f32[128]{0:T(128)S(1)}, f32[128]{0:T(128)}, u32[]{:S(2)}) copy-start(f32[128]{0:T(128)} %param.42) | copy-start | bytes 1540
  82.7 62.7 %all-gather.5.cloned.1.call-start = ((), (), s32[]{:S(2)}) async-start(), calls=%async_computation.1 | async-start | bytes 2621440 | tf_op jit(solution)/shard_map/all_gather | solution.py:131
  82.9 3.5 %copy-start.2 = (bf16[128,128,128]{2,1,0:T(8,128)(2,1)S(1)}, bf16[128,128,128]{2,1,0:T(8,128)(2,1)}, u32[]{:S(2)}) copy-start(bf16[128,128,128]{2,1,0:T(8,128)(2,1)} %param.31) | copy-start | bytes 12582916
  91.3 6.9 %copy-start.21 = (s32[512]{0:T(512)S(1)}, s32[512]{0:T(512)}, u32[]{:S(2)}) copy-start(s32[512]{0:T(512)} %param.35) | copy-start | bytes 6148
  91.3 6.9 %slice-start = ((bf16[128,2304]{1,0:T(8,128)(2,1)}), bf16[128,768]{1,0:T(8,128)(2,1)S(1)}, s32[]{:S(2)}) async-start(bf16[128,2304]{1,0:T(8,128)(2,1)} %copy-done.7), calls=%async_computation.2 | async-start | bytes 393216 | tf_op jit(solution)/shard_map/slice | solution.py:169
  98.2 50.6 %copy-start.23 = (pred[512]{0:T(512)(128)(4,1)}, pred[512]{0:T(512)(128)(4,1)S(1)}, u32[]{:S(2)}) copy-start(pred[512]{0:T(512)(128)(4,1)S(1)} %broadcast_compare_fusion.1) | copy-start | bytes 1540
  98.3 50.4 %copy-start.14 = (bf16[128,768]{0,1:T(8,128)(2,1)}, bf16[128,768]{0,1:T(8,128)(2,1)S(1)}, u32[]{:S(2)}) copy-start(bf16[128,768]{0,1:T(8,128)(2,1)S(1)} %copy.82) | copy-start | bytes 589828
  148.7 4.5 %copy-start.6 = (f32[128,768]{1,0:T(8,128)S(1)}, f32[128,768]{1,0:T(8,128)}, u32[]{:S(2)}) copy-start(f32[128,768]{1,0:T(8,128)} %get-tuple-element.50) | copy-start | bytes 1179652
  148.8 4.5 %copy-start.11 = (bf16[768,768]{1,0:T(8,128)(2,1)S(1)}, bf16[768,768]{1,0:T(8,128)(2,1)}, u32[]{:S(2)}) copy-start(bf16[768,768]{1,0:T(8,128)(2,1)} %param.46) | copy-start | bytes 3538948
  154.6 3.5 %copy-start.24 = (bf16[1536,768]{1,0:T(8,128)(2,1)S(1)}, bf16[1536,768]{1,0:T(8,128)(2,1)}, u32[]{:S(2)}) copy-start(bf16[1536,768]{1,0:T(8,128)(2,1)} %param.48) | copy-start | bytes 7077892
  158.2 1.0 copy-start.9
  158.2 1.1 copy-start.12
  158.2 2.0 copy-start.22
  158.2 11.5 %copy-start.15 = (bf16[2,128,384]{2,1,0:T(8,128)(2,1)S(1)}, bf16[2,128,384]{2,1,0:T(8,128)(2,1)}, u32[]{:S(2)}) copy-start(bf16[2,128,384]{2,1,0:T(8,128)(2,1)} %param.38) | copy-start | bytes 589828
  159.3 10.8 %copy-start.13 = (bf16[128,768]{1,0:T(8,128)(2,1)}, bf16[128,768]{1,0:T(8,128)(2,1)S(1)}, u32[]{:S(2)}) copy-start(bf16[128,768]{1,0:T(8,128)(2,1)S(1)} %fusion.41) | copy-start | bytes 589828
  159.8 5.8 %copy-start.4 = (f32[1024,128]{1,0:T(8,128)}, f32[1024,128]{1,0:T(8,128)S(1)}, u32[]{:S(2)}) copy-start(f32[1024,128]{1,0:T(8,128)S(1)} %get-tuple-element.54) | copy-start | bytes 1572868
  160.6 5.0 %collective-permute-start.2 = (bf16[96,128]{1,0:T(8,128)(2,1)S(1)}, bf16[96,128]{1,0:T(8,128)(2,1)S(1)}, u32[]{:S(2)}, u32[]{:S(2)}) collective-permute-start(bf16[96,128]{1,0:T(8,128)(2,1)S(1)} %get-tuple-element.30), channel_id=1, source_target_pairs={{0,1},{1,2},{2,3},{4,5},{5,6},{6,7},{8,9},{9,10},{10,11},{12,13},{... | collective-permute-start | bytes 73736 | tf_op jit(solution)/shard_map/ppermute | solution.py:26
  164.0 5.7 %collective-permute-start.3 = (bf16[96,128]{1,0:T(8,128)(2,1)S(1)}, bf16[96,128]{1,0:T(8,128)(2,1)S(1)}, u32[]{:S(2)}, u32[]{:S(2)}) collective-permute-start(bf16[96,128]{1,0:T(8,128)(2,1)S(1)} %get-tuple-element.31), channel_id=1, source_target_pairs={{1,0},{2,1},{3,2},{5,4},{6,5},{7,6},{9,8},{10,9},{11,10},{13,12},{... | collective-permute-start | bytes 73736 | tf_op jit(solution)/shard_map/ppermute | solution.py:29
  176.8 0.7 copy-start.18
  176.8 0.7 copy-start.20
  177.5 4.3 %copy-start.5 = (bf16[32,224,128]{2,1,0:T(8,128)(2,1)S(1)}, bf16[32,224,128]{2,1,0:T(8,128)(2,1)}, u32[]{:S(2)}) copy-start(bf16[32,224,128]{2,1,0:T(8,128)(2,1)} %get-tuple-element.11) | copy-start | bytes 5505028
  184.9 12.2 %copy-start.1 = (bf16[768,2304]{1,0:T(8,128)(2,1)S(1)}, bf16[768,2304]{1,0:T(8,128)(2,1)}, u32[]{:S(2)}) copy-start(bf16[768,2304]{1,0:T(8,128)(2,1)} %param.45) | copy-start | bytes 10616836
  188.7 6.6 %copy-start.16 = (f32[1,3,1024]{2,0,1:T(1,128)S(1)}, f32[1,3,1024]{2,0,1:T(1,128)}, u32[]{:S(2)}) copy-start(f32[1,3,1024]{2,0,1:T(1,128)} %param.27) | copy-start | bytes 36868
  188.7 6.6 %copy-start.26 = (bf16[3,128]{1,0:T(4,128)(2,1)S(1)}, bf16[3,128]{1,0:T(4,128)(2,1)}, u32[]{:S(2)}) copy-start(bf16[3,128]{1,0:T(4,128)(2,1)} %param.51) | copy-start | bytes 2308
Sparse Core Ops, SparseCore 0:
  82.8 39.2 all-gather.2
  123.7 21.6 all-gather.4
where the time goes:
time: 205 us; the launch traced here: 204 us
  local copies, waits for them, and re-layouts  56.3 us (27%)
  waiting for transfers between devices  49.1 us (24%)
  matrix products  41.6 us (20%)
  other arithmetic  29 us (14%)
  between operations  15.9 us (8%)
  starting transfers between devices  12 us (6%)
    all_gather x1, waiting for transfers between devices, per_device(): gathered = lax.all_gather(projected[:, D:], 'row', axis=0, tiled=True)  23.7 us
    all_gather x1, waiting for transfers between devices, per_device(): lax.all_gather(pair_bias_of(pair_cond, pair_gain, pair_heads), 'smp', axi...  21.2 us
    slice x4, local copies, waits for them, and re-layouts, window_attend(): windows[:, :, :CA].reshape(block_count, span_rows, AHEADS, head_size)  12.1 us
    sub x2, other arithmetic, softmax_rows(): exponent = jnp.exp(scores - largest)  10.7 us
    another operation x10, local copies, waits for them, and re-layouts, block_spans(): jnp.stack(pieces, axis=1)  10.6 us
    ppermute x2, starting transfers between devices, with_halo(): lax.ppermute(lax.slice_in_dim(block, block.shape[dim] - width, None, axis...  8.95 us
    reduce_sum x6, other arithmetic, layer_norm(): variance = jnp.mean(centred * centred, axis=-1, keepdims=True)  7.22 us
    slice x2, local copies, waits for them, and re-layouts, window_attend(): windows[:, :, CA:].reshape(block_count, span_rows, AHEADS, head_size)  7.01 us
  transfers between devices with their start and end apart: 6, of which 3 were waited for; matrix products, arithmetic and copies ran while one was open for 19% of the time, Pallas kernels for 0%

commit v1 on v0

--- a/solution.py
+++ b/solution.py
@@ -16,6 +16,18 @@
 norm_eps = 1e-05
 masked_score = -1e30
 outside_score = -2e30
+
+
+def collect(x, axis, dim):
+    ways, here, step = (lax.axis_size(axis), lax.axis_index(axis), x.shape[dim])
+    line, have = (x, 1)
+    while have < ways:
+        line = jnp.concatenate(
+            [line, lax.ppermute(line, axis, [(d, (d - have) % ways) for d in range(ways)])],
+            axis=dim,
+        )
+        have = 2 * have
+    return jnp.roll(line, here * step, axis=dim)
 
 
 def with_halo(block, sides, width):
@@ -164,7 +176,7 @@
     )
     normed = layer_norm(token_state, token_gain[0]).astype(jnp.bfloat16)
     projected = jnp.dot(normed, token_qkv, preferred_element_type=jnp.float32).astype(jnp.bfloat16)
-    gathered = lax.all_gather(projected[:, D:], "row", axis=0, tiled=True)
+    gathered = collect(projected[:, D:], "row", 0)
     key_count = gathered.shape[0]
     query_heads = projected[:, :D].reshape(tok_rows, HEADS, head_size)
     key_heads = gathered[:, :D].reshape(key_count, HEADS, head_size)

time: 205 us -> 209 us (1.020)
  waiting for transfers between devices: 49.1 us -> 43.2 us
  local copies, waits for them, and re-layouts: 56.3 us -> 61.3 us
  starting transfers between devices: 12 us -> 15.9 us
    ppermute x0 -> x2, waiting for transfers between devices: none -> 39 us  [collect(): lax.ppermute(line, axis, [(d, (d - have) % ways) for d in range(ways)])]
    all_gather x1 -> x0, waiting for transfers between devices: 23.7 us -> none  [per_device(): gathered = lax.all_gather(projected[:, D:], 'row', axis=0, tiled=True)]
    all_gather x1, waiting for transfers between devices: 21.2 us -> 0.02 us  [per_device(): lax.all_gather(pair_bias_of(pair_cond, pair_gain, pair_heads), 'smp', axi...]
    ppermute x0 -> x2, starting transfers between devices: none -> 5.84 us  [collect(): lax.ppermute(line, axis, [(d, (d - have) % ways) for d in range(ways)])]
    unnamed x69 -> x75, local copies, waits for them, and re-layouts: 3.11 us -> 6.42 us
  transfers between devices with their start and end apart: 6 -> 7, of which waited for: 3 -> 3; matrix products, arithmetic and copies ran while one was open for 19% -> 40% of each run, Pallas kernels for 0% -> 0%
where the time goes in v1:
time: 209 us; the launch traced here: 208 us
  local copies, waits for them, and re-layouts  61.3 us (29%)
  waiting for transfers between devices  43.2 us (21%)
  matrix products  41.7 us (20%)
  other arithmetic  29.6 us (14%)
  starting transfers between devices  15.9 us (8%)
  between operations  15.8 us (8%)
    ppermute x2, waiting for transfers between devices, collect(): lax.ppermute(line, axis, [(d, (d - have) % ways) for d in range(ways)])  39 us
    slice x4, local copies, waits for them, and re-layouts, window_attend(): windows[:, :, :CA].reshape(block_count, span_rows, AHEADS, head_size)  12.2 us
    another operation x10, local copies, waits for them, and re-layouts, block_spans(): jnp.stack(pieces, axis=1)  10.7 us
    sub x2, other arithmetic, softmax_rows(): exponent = jnp.exp(scores - largest)  10.7 us
    reduce_sum x6, other arithmetic, layer_norm(): variance = jnp.mean(centred * centred, axis=-1, keepdims=True)  7.22 us
    ppermute x2, starting transfers between devices, with_halo(): lax.ppermute(lax.slice_in_dim(block, block.shape[dim] - width, None, axis...  7.12 us
    slice x2, local copies, waits for them, and re-layouts, window_attend(): windows[:, :, CA:].reshape(block_count, span_rows, AHEADS, head_size)  7.02 us
    unnamed x75, local copies, waits for them, and re-layouts  6.42 us
  transfers between devices with their start and end apart: 7, of which 3 were waited for; matrix products, arithmetic and copies ran while one was open for 40% of the time, Pallas kernels for 0%

profile of v1, /device:TPU:0, one launch (start us, length us, event | category | flops | bytes accessed | tf_op | source)
XLA Modules:
  0.0 207.5 jit_solution(9405036323727527090)
XLA Ops:
  8.1 2.2 %fusion.123 = (f32[1024]{0:T(1024)S(1)}, f32[1024,128]{1,0:T(8,128)S(1)}) fusion(f32[3,128]{1,0:T(4,128)} %param.36, f32[]{:T(128)S(6)} %sqrt.8, f32[1,3,1024]{2,0,1:T(1,128)} %param.27, f32[]{:T(128)S(6)} %sqrt.7, f32[1,3,1024]{2,0,1:T(1,128)} %param.26, bf16[1024,128]{1,0:T(8,128)(2,1)} %param.29), kind=kOutput, calls=%fused_computation.210 | convolution fusion | flops 5120000 | bytes 816648 | tf_op jit(solution)/shard_map/ka,kc->ac/dot_general | solution.py:162
  10.8 1.3 slice_bitcast_fusion
  13.7 5.6 %collective-permute-start = (bf16[96,128]{1,0:T(8,128)(2,1)}, bf16[96,128]{1,0:T(8,128)(2,1)}, u32[]{:S(2)}, u32[]{:S(2)}) collective-permute-start(bf16[96,128]{1,0:T(8,128)(2,1)} %get-tuple-element.34), channel_id=1, source_target_pairs={{0,1},{1,2},{2,3},{4,5},{5,6},{6,7},{8,9},{9,10},{10,11},{12,13},{... | collective-permute-start | bytes 73736 | tf_op jit(solution)/shard_map/ppermute | solution.py:38
  19.3 1.4 collective-permute-start.1
  20.7 3.4 %convert_reduce_fusion = f32[128,128]{1,0:T(8,128)S(1)} fusion(bf16[128,128,128]{2,1,0:T(8,128)(2,1)} %param.31), kind=kLoop, calls=%fused_computation.4 | loop fusion | flops 4177920 | bytes 4259840 | tf_op jit(solution)/shard_map/reduce_sum | solution.py:47
  24.1 4.8 %fusion.5 = f32[128,128]{1,0:T(8,128)S(1)} fusion(bf16[128,128,128]{2,1,0:T(8,128)(2,1)S(1)} %copy-done.2, f32[128,128]{1,0:T(8,128)S(1)} %broadcast_multiply_fusion), kind=kLoop, calls=%fused_computation.7 | loop fusion | flops 8372224 | bytes 4325376 | tf_op jit(solution)/shard_map/reduce_sum | solution.py:49
  28.9 5.9 %fusion.8 = bf16[128,128,16]{1,2,0:T(8,128)(2,1)S(1)} fusion(bf16[128,128,128]{2,1,0:T(8,128)(2,1)S(1)} %copy-done.2, f32[128]{0:T(128)S(1)} %copy-done.28, f32[128,128]{1,0:T(8,128)S(1)} %add_rsqrt_fusion, f32[128,128]{1,0:T(8,128)S(1)} %broadcast_multiply_fusion, bf16[128,16]{0,1:T(8,128)(2,1)S(1)} %copy-done.26), kind=kOutput, calls=%fused_computation.10 | convolution fusion | flops 77594624 | bytes 4854272 | tf_op jit(solution)/shard_map/ijc,ch->hij/dot_general | solution.py:61
  34.8 1.0 copy.124
  36.5 0.8 stack.88
  37.3 1.4 stack.89
  38.6 1.4 stack.90
  40.0 1.4 stack.91
  41.4 1.4 stack.92
  42.7 1.4 stack.93
  44.1 1.4 stack.94
  45.5 1.7 stack.95
  47.1 1.5 broadcast_compare_fusion
  52.1 1.3 broadcast_multiply_fusion.1
  53.4 0.8 slice_reduce_fusion
  54.2 1.5 gt.27
  55.7 1.4 convolution_convert_fusion.2
  58.4 2.6 %fusion.117 = (bf16[32,224,128]{2,1,0:T(8,128)(2,1)}, bf16[32,224,128]{2,1,0:T(8,128)(2,1)}) fusion(bf16[32,224,256]{2,1,0:T(8,128)(2,1)S(1)} %bitcast.141), kind=kLoop, calls=%fused_computation.204 | loop fusion | bytes 7340032 | tf_op jit(solution)/shard_map/slice | solution.py:78
  60.9 4.0 %copy.78 = bf16[32,224,128]{1,2,0:T(8,128)(2,1)} copy(bf16[32,224,128]{2,1,0:T(8,128)(2,1)} %get-tuple-element.12) | data formatting | bytes 3670016 | tf_op jit(solution)/shard_map/slice | solution.py:78
  64.9 2.8 %reshape.297 = bf16[32,32,4,32]{3,2,1,0:T(4,128)(2,1)} reshape(bf16[1024,128]{1,0:T(8,128)(2,1)} %slice.290) | data formatting | bytes 524288 | tf_op jit(solution)/shard_map/reshape | solution.py:77
  67.7 4.0 %copy.77 = bf16[32,224,128]{1,2,0:T(8,128)(2,1)} copy(bf16[32,224,128]{2,1,0:T(8,128)(2,1)} %get-tuple-element.13) | data formatting | bytes 3670016 | tf_op jit(solution)/shard_map/slice | solution.py:79
  71.6 2.6 %fusion.49 = f32[32,4,32,224]{3,2,1,0:T(8,128)S(1)} fusion(bf16[32,224,4,32]{1,3,2,0:T(8,128)(2,1)} %bitcast.139, bf16[32,32,4,32]{3,2,1,0:T(4,128)(2,1)} %reshape.297), kind=kOutput, calls=%fused_computation.72 | convolution fusion | flops 58720256 | bytes 5767168 | tf_op jit(solution)/shard_map/bqhd,bkhd->bhqk/dot_general | solution.py:80
  74.3 6.4 %fusion.124 = (f32[32,4,32]{2,1,0:T(4,128)S(1)}, f32[32,4,32,224]{3,2,1,0:T(8,128)S(1)}) fusion(f32[32,4,32,224]{3,2,1,0:T(8,128)S(1)} %fusion.49, pred[32,224]{1,0:T(8,128)(4,1)S(1)} %copy-done.20, pred[32,224]{1,0:T(8,128)(4,1)S(1)} %copy-done.22), kind=kOutput, calls=%fused_computation.211 | output fusion | flops 7340255 | bytes 7370752 | tf_op jit(solution)/shard_map/sub | solution.py:55
  80.7 1.0 fusion.35
  81.8 1.7 copy.80
  83.4 2.9 %reshape.299 = bf16[1024,128]{0,1:T(8,128)(2,1)} reshape(bf16[32,32,4,32]{1,0,3,2:T(8,128)(2,1)} %copy.80) | data formatting | bytes 524288 | tf_op jit(solution)/shard_map/reshape | solution.py:90
  86.4 2.2 %convolution_add_fusion.2 = f32[1024,128]{1,0:T(8,128)} fusion(f32[1024,128]{1,0:T(8,128)} %copy-done.3, bf16[1024,128]{0,1:T(8,128)(2,1)} %reshape.299, bf16[2,128,128]{2,1,0:T(8,128)(2,1)} %param.39), kind=kOutput, calls=%fused_computation.53 | convolution fusion | flops 33685504 | bytes 1343488 | tf_op jit(solution)/shard_map/dot_general | solution.py:89
  88.5 3.4 %fusion.125 = (f32[128]{0:T(128)}, f32[128,768]{1,0:T(8,128)}) fusion(f32[768]{0:T(1024)} %broadcast_multiply_fusion.1, bf16[128,768]{1,0:T(8,128)(2,1)} %param.30, f32[128]{0:T(128)} %broadcast_maximum_fusion, bf16[128,768]{1,0:T(8,128)(2,1)} %param.40, f32[1024,128]{1,0:T(8,128)} %convolution_add_fusion.2, s32[1024]{0:T(1024)S(1)} %broadcast_subtract_fusion, ...), kind=kOutput, calls=%fused_computation.212 | convolution fusion | flops 405110656 | bytes 1319936 | tf_op jit(solution)/shard_map/dot_general | solution.py:171
  92.6 1.2 multiply_reduce_fusion.4
  93.8 1.7 convolution_convert_fusion
  95.5 0.8 copy-done.6
  96.3 0.8 fusion.120
  97.1 4.5 %collective-permute-start.2 = (bf16[128,1536]{1,0:T(8,128)(2,1)S(1)}, bf16[128,1536]{1,0:T(8,128)(2,1)S(1)}, u32[]{:S(2)}, u32[]{:S(2)}) collective-permute-start(bf16[128,1536]{1,0:T(8,128)(2,1)S(1)} %get-tuple-element.30), channel_id=1, source_target_pairs={{0,3},{1,0},{2,1},{3,2},{4,7},{5,4},{6,5},{7,6},{8,11},{9,8},{10,9... | collective-permute-start | bytes 1179656 | tf_op jit(solution)/shard_map/ppermute | solution.py:26
  101.6 7.9 %collective-permute-done.2 = bf16[128,1536]{1,0:T(8,128)(2,1)S(1)} collective-permute-done((bf16[128,1536]{1,0:T(8,128)(2,1)S(1)}, bf16[128,1536]{1,0:T(8,128)(2,1)S(1)}, u32[]{:S(2)}, u32[]{:S(2)}) %collective-permute-start.2) | collective-permute-done | bytes 393248 | tf_op jit(solution)/shard_map/ppermute | solution.py:26
  109.5 1.4 collective-permute-start.3
  111.6 0.9 slice.293
  112.5 0.8 copy.82
  113.3 0.8 constant_dynamic-update-slice_fusion.11
  114.1 31.2 %collective-permute-done.3 = bf16[256,1536]{1,0:T(8,128)(2,1)S(1)} collective-permute-done((bf16[256,1536]{1,0:T(8,128)(2,1)S(1)}, bf16[256,1536]{1,0:T(8,128)(2,1)S(1)}, u32[]{:S(2)}, u32[]{:S(2)}) %collective-permute-start.3) | collective-permute-done | bytes 786464 | tf_op jit(solution)/shard_map/ppermute | solution.py:26
  145.2 1.0 constant_dynamic-update-slice_fusion.10
  146.2 0.8 constant_dynamic-update-slice_fusion.9
  147.0 0.8 constant_dynamic-update-slice_fusion.8
  147.8 0.9 constant_dynamic-update-slice_fusion.7
  148.7 1.5 constant_dynamic-slice_fusion
  150.8 3.4 %fusion.128 = f32[16,128]{1,0:T(8,128)S(1)} fusion(bf16[16,128,512]{2,1,0:T(8,128)(2,1)} %all-gather.2.cloned.1.call-done, pred[512]{0:T(512)(128)(4,1)S(1)} %broadcast_compare_fusion.1, bf16[128,16,48]{0,2,1:T(8,128)(2,1)S(1)} %bitcast.165, bf16[512,16,48]{0,2,1:T(8,128)(2,1)S(1)} %bitcast.160), kind=kOutput, calls=%fused_computation.213 | convolution fusion | flops 106955264 | bytes 3088896 | tf_op jit(solution)/shard_map/sub | solution.py:55
  154.2 4.5 %fusion.40 = bf16[16,48,128]{2,1,0:T(8,128)(2,1)} fusion(bf16[512,16,48]{0,2,1:T(8,128)(2,1)S(1)} %bitcast.162, f32[16,128]{1,0:T(8,128)S(1)} %fusion.128, bf16[16,128,512]{2,1,0:T(8,128)(2,1)} %all-gather.2.cloned.1.call-done, pred[512]{0:T(512)(128)(4,1)S(1)} %broadcast_compare_fusion.1, bf16[128,16,48]{0,2,1:T(8,128)(2,1)S(1)} %bitcast.166, ...), kind=kOutput, calls=%fused_computation.60 | convolution fusion | flops 208767488 | bytes 4071936 | tf_op jit(solution)/shard_map/hij,jhd->ihd/dot_general | solution.py:191
  158.7 1.4 fusion.129
  160.3 3.3 %fusion.79 = f32[128,3072]{1,0:T(8,128)S(1)} fusion(bf16[768,3072]{1,0:T(8,128)(2,1)} %param.47, f32[128,768]{1,0:T(8,128)S(1)} %get-tuple-element.54, f32[768]{0:T(1024)S(1)} %get-tuple-element.8, f32[128]{0:T(128)S(1)} %add_rsqrt_fusion.4, f32[128]{0:T(128)S(1)} %broadcast_multiply_fusion.5), kind=kOutput, calls=%fused_computation.111 | convolution fusion | flops 604372992 | bytes 6688768 | tf_op jit(solution)/shard_map/dot_general | solution.py:197
  166.0 1.6 collective-permute-start.4
  167.6 1.5 collective-permute-start.5
  169.2 4.1 %collective-permute-done.5 = bf16[96,128]{1,0:T(8,128)(2,1)S(1)} collective-permute-done((bf16[96,128]{1,0:T(8,128)(2,1)S(1)}, bf16[96,128]{1,0:T(8,128)(2,1)S(1)}, u32[]{:S(2)}, u32[]{:S(2)}) %collective-permute-start.5) | collective-permute-done | bytes 24608 | tf_op jit(solution)/shard_map/ppermute | solution.py:41
  174.3 2.5 %fusion.116 = (bf16[32,224,128]{2,1,0:T(8,128)(2,1)}, bf16[32,224,128]{2,1,0:T(8,128)(2,1)}) fusion(bf16[32,224,256]{2,1,0:T(8,128)(2,1)S(1)} %bitcast.142), kind=kLoop, calls=%fused_computation.203 | loop fusion | bytes 7340032 | tf_op jit(solution)/shard_map/slice | solution.py:78
  176.8 3.2 %copy.93 = bf16[32,224,128]{1,2,0:T(8,128)(2,1)S(1)} copy(bf16[32,224,128]{2,1,0:T(8,128)(2,1)} %get-tuple-element.10) | data formatting | bytes 3670016 | tf_op jit(solution)/shard_map/slice | solution.py:78
  181.2 4.3 %fusion.131 = (f32[32,4,32]{2,1,0:T(4,128)}, f32[32,4,32,224]{3,2,1,0:T(8,128)}) fusion(f32[32,4,32,224]{3,2,1,0:T(8,128)S(1)} %fusion.47, pred[32,224]{1,0:T(8,128)(4,1)S(1)} %copy-done.21, pred[32,224]{1,0:T(8,128)(4,1)S(1)} %copy-done.23), kind=kOutput, calls=%fused_computation.216 | output fusion | flops 7340255 | bytes 7370752 | tf_op jit(solution)/shard_map/sub | solution.py:55
  185.4 3.1 %copy.92 = bf16[32,224,128]{1,2,0:T(8,128)(2,1)} copy(bf16[32,224,128]{2,1,0:T(8,128)(2,1)S(1)} %copy-done.5) | data formatting | bytes 3670016 | tf_op jit(solution)/shard_map/slice | solution.py:79
  188.5 3.8 %fusion.36 = bf16[32,32,4,32]{1,3,2,0:T(8,128)(2,1)S(1)} fusion(bf16[32,224,4,32]{1,3,2,0:T(8,128)(2,1)} %bitcast.159, f32[32,4,32,224]{3,2,1,0:T(8,128)} %get-tuple-element.58, f32[32,4,32]{2,1,0:T(4,128)} %get-tuple-element.57), kind=kOutput, calls=%fused_computation.50 | convolution fusion | flops 60686336 | bytes 5783552 | tf_op jit(solution)/shard_map/bhqk,bkhd->bqhd/dot_general | solution.py:86
  192.3 1.7 copy.95
  194.0 2.9 %reshape.308 = bf16[1024,128]{0,1:T(8,128)(2,1)} reshape(bf16[32,32,4,32]{1,0,3,2:T(8,128)(2,1)} %copy.95) | data formatting | bytes 524288 | tf_op jit(solution)/shard_map/reshape | solution.py:90
  196.9 1.6 fusion.132
  198.9 1.2 fusion.46
  (118 shorter events, 15.1 us)
Async XLA Ops:
  7.2 86.6 %copy-start = (bf16[768,2304]{1,0:T(8,128)(2,1)S(1)}, bf16[768,2304]{1,0:T(8,128)(2,1)}, u32[]{:S(2)}) copy-start(bf16[768,2304]{1,0:T(8,128)(2,1)} %param.45) | copy-start | bytes 10616836
  7.2 143.6 %all-gather.2.cloned.1.call-start = ((), (), s32[]{:S(2)}) async-start(), calls=%async_computation | async-start | bytes 2621440 | tf_op jit(solution)/shard_map/all_gather | solution.py:143
  8.1 15.9 %copy-start.2 = (bf16[128,128,128]{2,1,0:T(8,128)(2,1)S(1)}, bf16[128,128,128]{2,1,0:T(8,128)(2,1)}, u32[]{:S(2)}) copy-start(bf16[128,128,128]{2,1,0:T(8,128)(2,1)} %param.31) | copy-start | bytes 12582916
  10.4 1.7 copy-start.3
  12.4 0.7 copy-start.11
  13.7 42.0 %collective-permute-start = (bf16[96,128]{1,0:T(8,128)(2,1)}, bf16[96,128]{1,0:T(8,128)(2,1)}, u32[]{:S(2)}, u32[]{:S(2)}) collective-permute-start(bf16[96,128]{1,0:T(8,128)(2,1)} %get-tuple-element.34), channel_id=1, source_target_pairs={{0,1},{1,2},{2,3},{4,5},{5,6},{6,7},{8,9},{9,10},{10,11},{12,13},{... | collective-permute-start | bytes 73736 | tf_op jit(solution)/shard_map/ppermute | solution.py:38
  19.3 9.6 %copy-start.26 = (bf16[128,16]{0,1:T(8,128)(2,1)S(1)}, bf16[128,16]{0,1:T(8,128)(2,1)}, u32[]{:S(2)}) copy-start(bf16[128,16]{0,1:T(8,128)(2,1)} %param.43) | copy-start | bytes 12292
  19.3 9.6 %copy-start.28 = (f32[128]{0:T(128)S(1)}, f32[128]{0:T(128)}, u32[]{:S(2)}) copy-start(f32[128]{0:T(128)} %param.42) | copy-start | bytes 1540
  19.3 36.4 %collective-permute-start.1 = (bf16[96,128]{1,0:T(8,128)(2,1)}, bf16[96,128]{1,0:T(8,128)(2,1)}, u32[]{:S(2)}, u32[]{:S(2)}) collective-permute-start(bf16[96,128]{1,0:T(8,128)(2,1)} %get-tuple-element.35), channel_id=1, source_target_pairs={{1,0},{2,1},{3,2},{5,4},{6,5},{7,6},{9,8},{10,9},{11,10},{13,12},{... | collective-permute-start | bytes 73736 | tf_op jit(solution)/shard_map/ppermute | solution.py:41
  28.9 6.9 %copy-start.18 = (s32[4096]{0:T(1024)S(1)}, s32[4096]{0:T(1024)}, u32[]{:S(2)}) copy-start(s32[4096]{0:T(1024)} %param.34) | copy-start | bytes 49156
  71.6 2.6 %copy-start.20 = (pred[32,224]{1,0:T(8,128)(4,1)S(1)}, pred[32,224]{1,0:T(8,128)(4,1)}, u32[]{:S(2)}) copy-start(pred[32,224]{1,0:T(8,128)(4,1)} %gt.27) | copy-start | bytes 21508
  71.6 2.6 %copy-start.22 = (pred[32,224]{1,0:T(8,128)(4,1)S(1)}, pred[32,224]{1,0:T(8,128)(4,1)}, u32[]{:S(2)}) copy-start(pred[32,224]{1,0:T(8,128)(4,1)} %fusion.94) | copy-start | bytes 21508
  74.3 6.4 %copy-start.9 = (bf16[32,224,128]{1,2,0:T(8,128)(2,1)S(1)}, bf16[32,224,128]{1,2,0:T(8,128)(2,1)}, u32[]{:S(2)}) copy-start(bf16[32,224,128]{1,2,0:T(8,128)(2,1)} %copy.77) | copy-start | bytes 5505028
  95.5 0.8 copy-start.6
  97.1 49.1 %copy-start.7 = (bf16[128,2304]{1,0:T(8,128)(2,1)S(1)}, bf16[128,2304]{1,0:T(8,128)(2,1)}, u32[]{:S(2)}) copy-start(bf16[128,2304]{1,0:T(8,128)(2,1)} %copy-done.6) | copy-start | bytes 1769476
  97.1 12.3 %collective-permute-start.2 = (bf16[128,1536]{1,0:T(8,128)(2,1)S(1)}, bf16[128,1536]{1,0:T(8,128)(2,1)S(1)}, u32[]{:S(2)}, u32[]{:S(2)}) collective-permute-start(bf16[128,1536]{1,0:T(8,128)(2,1)S(1)} %get-tuple-element.30), channel_id=1, source_target_pairs={{0,3},{1,0},{2,1},{3,2},{4,7},{5,4},{6,5},{7,6},{8,11},{9,8},{10,9... | collective-permute-start | bytes 1179656 | tf_op jit(solution)/shard_map/ppermute | solution.py:26
  109.5 35.7 %collective-permute-start.3 = (bf16[256,1536]{1,0:T(8,128)(2,1)S(1)}, bf16[256,1536]{1,0:T(8,128)(2,1)S(1)}, u32[]{:S(2)}, u32[]{:S(2)}) collective-permute-start(bf16[256,1536]{1,0:T(8,128)(2,1)S(1)} %pad_maximum_fusion), channel_id=1, source_target_pairs={{0,2},{1,3},{2,0},{3,1},{4,6},{5,7},{6,4},{7,5},{8,10},{9,11},{10,... | collective-permute-start | bytes 2359304 | tf_op jit(solution)/shard_map/ppermute | solution.py:26
  147.8 3.0 %copy-start.15 = (bf16[128,768]{0,1:T(8,128)(2,1)S(1)}, bf16[128,768]{0,1:T(8,128)(2,1)}, u32[]{:S(2)}) copy-start(bf16[128,768]{0,1:T(8,128)(2,1)} %copy.82) | copy-start | bytes 589828
  150.8 3.4 %copy-start.16 = (bf16[128,768]{0,1:T(8,128)(2,1)S(1)}, bf16[128,768]{0,1:T(8,128)(2,1)}, u32[]{:S(2)}) copy-start(bf16[128,768]{0,1:T(8,128)(2,1)} %copy.82) | copy-start | bytes 589828
  154.2 4.5 %copy-start.8 = (f32[128,768]{1,0:T(8,128)S(1)}, f32[128,768]{1,0:T(8,128)}, u32[]{:S(2)}) copy-start(f32[128,768]{1,0:T(8,128)} %get-tuple-element.52) | copy-start | bytes 1179652
  154.2 4.5 %copy-start.12 = (bf16[768,768]{1,0:T(8,128)(2,1)S(1)}, bf16[768,768]{1,0:T(8,128)(2,1)}, u32[]{:S(2)}) copy-start(bf16[768,768]{1,0:T(8,128)(2,1)} %param.46) | copy-start | bytes 3538948
  160.1 3.5 %copy-start.25 = (bf16[1536,768]{1,0:T(8,128)(2,1)S(1)}, bf16[1536,768]{1,0:T(8,128)(2,1)}, u32[]{:S(2)}) copy-start(bf16[1536,768]{1,0:T(8,128)(2,1)} %param.48) | copy-start | bytes 7077892
  163.6 1.0 copy-start.10
  163.6 1.1 copy-start.13
  163.6 2.0 copy-start.24
  163.6 9.7 %copy-start.17 = (bf16[2,128,384]{2,1,0:T(8,128)(2,1)S(1)}, bf16[2,128,384]{2,1,0:T(8,128)(2,1)}, u32[]{:S(2)}) copy-start(bf16[2,128,384]{2,1,0:T(8,128)(2,1)} %param.38) | copy-start | bytes 589828
  164.7 9.0 %copy-start.14 = (bf16[128,768]{1,0:T(8,128)(2,1)}, bf16[128,768]{1,0:T(8,128)(2,1)S(1)}, u32[]{:S(2)}) copy-start(bf16[128,768]{1,0:T(8,128)(2,1)S(1)} %fusion.41) | copy-start | bytes 589828
  165.3 4.0 %copy-start.4 = (f32[1024,128]{1,0:T(8,128)}, f32[1024,128]{1,0:T(8,128)S(1)}, u32[]{:S(2)}) copy-start(f32[1024,128]{1,0:T(8,128)S(1)} %get-tuple-element.56) | copy-start | bytes 1572868
  166.0 3.2 %collective-permute-start.4 = (bf16[96,128]{1,0:T(8,128)(2,1)S(1)}, bf16[96,128]{1,0:T(8,128)(2,1)S(1)}, u32[]{:S(2)}, u32[]{:S(2)}) collective-permute-start(bf16[96,128]{1,0:T(8,128)(2,1)S(1)} %get-tuple-element.32), channel_id=1, source_target_pairs={{0,1},{1,2},{2,3},{4,5},{5,6},{6,7},{8,9},{9,10},{10,11},{12,13},{... | collective-permute-start | bytes 73736 | tf_op jit(solution)/shard_map/ppermute | solution.py:38
  167.6 5.7 %collective-permute-start.5 = (bf16[96,128]{1,0:T(8,128)(2,1)S(1)}, bf16[96,128]{1,0:T(8,128)(2,1)S(1)}, u32[]{:S(2)}, u32[]{:S(2)}) collective-permute-start(bf16[96,128]{1,0:T(8,128)(2,1)S(1)} %get-tuple-element.33), channel_id=1, source_target_pairs={{1,0},{2,1},{3,2},{5,4},{6,5},{7,6},{9,8},{10,9},{11,10},{13,12},{... | collective-permute-start | bytes 73736 | tf_op jit(solution)/shard_map/ppermute | solution.py:41
  180.4 0.7 copy-start.21
  180.4 0.7 copy-start.23
  181.1 4.3 %copy-start.5 = (bf16[32,224,128]{2,1,0:T(8,128)(2,1)S(1)}, bf16[32,224,128]{2,1,0:T(8,128)(2,1)}, u32[]{:S(2)}) copy-start(bf16[32,224,128]{2,1,0:T(8,128)(2,1)} %get-tuple-element.11) | copy-start | bytes 5505028
  188.5 12.2 %copy-start.1 = (bf16[768,2304]{1,0:T(8,128)(2,1)S(1)}, bf16[768,2304]{1,0:T(8,128)(2,1)}, u32[]{:S(2)}) copy-start(bf16[768,2304]{1,0:T(8,128)(2,1)} %param.45) | copy-start | bytes 10616836
  192.3 6.6 %copy-start.19 = (f32[1,3,1024]{2,0,1:T(1,128)S(1)}, f32[1,3,1024]{2,0,1:T(1,128)}, u32[]{:S(2)}) copy-start(f32[1,3,1024]{2,0,1:T(1,128)} %param.27) | copy-start | bytes 36868
  192.3 6.6 %copy-start.27 = (bf16[3,128]{1,0:T(4,128)(2,1)S(1)}, bf16[3,128]{1,0:T(4,128)(2,1)}, u32[]{:S(2)}) copy-start(bf16[3,128]{1,0:T(4,128)(2,1)} %param.51) | copy-start | bytes 2308
Sparse Core Ops, SparseCore 0:
  35.9 25.0 all-gather.1
